TPU v7x, 512 devices: a whole 4x4x16 slice. The times are simulated.
512 devices in a mesh: wide: 64 (over x, y, z_hi), grp: 8 (over z_lo, core).
Axes of the slice: x: 4, y: 4, z: 16 (z_hi: 4, z_lo: 4; z = z_hi * 4 + z_lo), core: 2. Of those that a mesh axis runs over, the one named last changes fastest.
Arguments:
- samples: bfloat16 [2048, 512], P(('wide', 'grp')), may hold values from -6 to 6
- archive: bfloat16 [262144, 512], P(('wide', 'grp')), may hold values from -6 to 6
- inv_len: float32 [512], replicated, may hold values from 0.7 to 2.8
- mean_coef: bfloat16 [262144, 64], P(('wide', 'grp')), may hold values from -0.1875 to 0.1875
- var_coef: bfloat16 [262144, 64], P(('wide', 'grp')), may hold values from -1 to 1
Outputs:
- pred_mean: float32 [2048, 64], P(('wide', 'grp'))
- pred_var: float32 [2048, 64], P(('wide', 'grp'))
All inputs are finite; a program needn't handle non-finite values.
Results may differ from a plain program's by a relative error of at most 0.0085.
Values may be sent and summed in bfloat16 or wider, within the bound.
A program may use at most 64 MiB of HBM per device.

v0:
```python
import jax
import jax.numpy as jnp
from jax import lax
from jax.sharding import PartitionSpec as P

DIN = 512


def scaled_rows(rows, inv_len):
    factor = inv_len * DIN ** (-0.5)
    scaled = (rows.astype(jnp.float32) * factor).astype(jnp.bfloat16)
    wide_copy = scaled.astype(jnp.float32)
    return (scaled, jnp.sum(wide_copy * wide_copy, axis=-1))


def on_device(samples, archive, inv_len, mean_coef, var_coef):
    gathered = lax.all_gather(samples, ("wide", "grp"), axis=0, tiled=True)
    samp_z, samp_norm = scaled_rows(gathered, inv_len)
    arch_z, arch_norm = scaled_rows(archive, inv_len)
    local_runs = archive.shape[0]
    block_rows = min(128, local_runs)
    block_count = local_runs // block_rows
    width = mean_coef.shape[1]
    arch_blocks = arch_z.reshape(block_count, block_rows, DIN)
    norm_blocks = arch_norm.reshape(block_count, block_rows)
    mean_blocks = mean_coef.reshape(block_count, block_rows, width)
    var_blocks = var_coef.reshape(block_count, block_rows, width)
    own_rows = samples.shape[0]

    def accumulate(totals, pieces):
        mean_sum, corr_sum = totals
        block_z, block_norm, mean_rows, var_rows = pieces
        inner_prod = lax.dot_general(
            samp_z, block_z, (((1,), (1,)), ((), ())), preferred_element_type=jnp.float32
        )
        kernel = jnp.exp(inner_prod - 0.5 * samp_norm[:, None] - 0.5 * block_norm[None, :])
        kernel_half = kernel.astype(jnp.bfloat16)
        square_half = (kernel * kernel).astype(jnp.bfloat16)
        mean_sum = mean_sum + jnp.dot(kernel_half, mean_rows, preferred_element_type=jnp.float32)
        corr_sum = corr_sum + jnp.dot(square_half, var_rows, preferred_element_type=jnp.float32)
        return ((mean_sum, corr_sum), None)

    start_pair = (
        jnp.zeros((own_rows * lax.axis_size(("wide", "grp")), width), jnp.float32),
        jnp.zeros((own_rows * lax.axis_size(("wide", "grp")), width), jnp.float32),
    )
    final_pair, unused = lax.scan(
        accumulate, start_pair, (arch_blocks, norm_blocks, mean_blocks, var_blocks)
    )
    summed = lax.psum_scatter(
        jnp.concatenate([final_pair[0], final_pair[1]], axis=1),
        ("wide", "grp"),
        scatter_dimension=0,
        tiled=True,
    )
    pred_mean = summed[:, :width]
    pred_var = 1.0 - summed[:, width:]
    return (pred_mean, pred_var)


def solution(mesh):
    in_specs = (
        P(("wide", "grp"), None),
        P(("wide", "grp"), None),
        P(),
        P(("wide", "grp"), None),
        P(("wide", "grp"), None),
    )
    out_specs = (P(("wide", "grp"), None), P(("wide", "grp"), None))
    return jax.shard_map(
        on_device, mesh=mesh, in_specs=in_specs, out_specs=out_specs, check_vma=False
    )
```

profile of v0, /device:TPU:1, one launch (start us, length us, event | category | flops | bytes accessed | tf_op | source)
XLA Modules:
  0.0 715.8 jit_solution(6088330128535756338)
XLA Ops:
  7.2 0.0 all-gather.3.cloned.1.call-start
  7.2 0.7 all-gather.3.cloned.1.call-update
  7.9 0.0 all-reduce.3.cloned.1.call-start
  8.0 1.0 copy.11
  8.9 1.0 copy.12
  9.9 0.7 broadcast_multiply_fusion.1
  10.6 2.0 multiply_reduce_fusion.1
  12.6 199.4 %all-gather.3.cloned.1.call-done = bf16[512,4,512]{2,1,0:T(4,128)(2,1)} async-done(((bf16[1,4,512]{2,1,0:T(4,128)(2,1)}), bf16[512,4,512]{2,1,0:T(4,128)(2,1)}) %all-gather.3.cloned.1.call-update) | async-done | bytes 2097168 | tf_op jit(solution)/shard_map/all_gather | solution.py:17
  212.0 4.2 reshape.27
  216.2 2.8 multiply_reduce_fusion
  218.9 21.9 %while.13 = (s32[]{:T(128)}, f32[2048,64]{0,1:T(8,128)}, f32[2048,64]{0,1:T(8,128)}, bf16[4,128,512]{2,1,0:T(8,128)(2,1)}, bf16[2048,512]{1,0:T(8,128)(2,1)S(1)}...) while((s32[]{:T(128)}, f32[2048,64]{0,1:T(8,128)}, ...), condition=%wide.region_3.4_spmd.clone, body=%wide.region_2.3_spmd.clone.sunk | while | flops 337381504 | bytes 7563396 | solution.py:47
  219.0 1.7 fusion.28
  220.7 1.1 convolution_add_fusion.5
  221.8 1.1 convolution_add_fusion.4
  222.9 1.7 fusion.28
  224.6 2.1 convolution_add_fusion.5
  226.7 2.1 convolution_add_fusion.4
  228.9 1.7 fusion.28
  230.6 2.1 convolution_add_fusion.5
  232.7 2.1 convolution_add_fusion.4
  234.9 1.7 fusion.28
  236.6 2.1 convolution_add_fusion.5
  238.7 2.1 convolution_add_fusion.4
  240.8 1.4 copy.13
  242.2 1.4 copy.14
  243.6 1.4 pad_maximum_fusion
  245.0 0.0 all-reduce.3.cloned.1.call-update
  245.0 462.6 %all-reduce.3.cloned.1.call-done = f32[2048,128]{1,0:T(8,128)} async-done(((f32[2048,128]{1,0:T(8,128)}), f32[2048,128]{1,0:T(8,128)}) %all-reduce.3.cloned.1.call-update) | async-done | bytes 1048592
  707.6 0.7 constant_dynamic-slice_fusion.1
  708.3 0.7 slice_subtract_fusion
  (10 shorter events, 0.0 us)
Async XLA Ops:
  7.2 204.8 %all-gather.3.cloned.1.call-start = ((), (), s32[]{:S(2)}) async-start(), calls=%async_computation | async-start | bytes 2101248 | tf_op jit(solution)/shard_map/all_gather | solution.py:17
  7.9 699.7 %all-reduce.3.cloned.1.call-start = ((), (), s32[]{:S(2)}) async-start(), calls=%async_computation.1 | async-start | bytes 2097152
Sparse Core Ops, SparseCore 0:
  12.6 199.3 all-gather.2
  245.1 462.4 all-reduce.2
where the time goes:
time: 717 us; the launch traced here: 716 us
  waiting for transfers between devices  663 us (92%)
  matrix products  21.8 us (3%)
  between operations  14.1 us (2%)
  local copies, waits for them, and re-layouts  9.55 us (1%)
  other arithmetic  7.5 us (1%)
    unnamed x3, waiting for transfers between devices  463 us
    all_gather x1, waiting for transfers between devices, on_device(): gathered = lax.all_gather(samples, ('wide', 'grp'), axis=0, tiled=True)  199 us
  transfers between devices with their start and end apart: 2, of which 2 were waited for; matrix products, arithmetic and copies ran while one was open for 1% of the time, Pallas kernels for 0%

commit v1 on v0

v1 whole, which is shorter than its diff:
```python
import functools

import jax
import jax.numpy as jnp
from jax import lax
from jax.experimental import pallas as pl
from jax.experimental.pallas import tpu as pltpu
from jax.sharding import PartitionSpec as P

MESH = pl.DeviceIdType.MESH
F32 = jnp.float32
BF16 = jnp.bfloat16
DIN = 512
OUT = 64
ROWS = 4
RUNS = 512
NX, NY, NZ, NC = 4, 4, 16, 2
Z_SLOTS = (0, 1, -1, 2, -2, 3, -3, 4, -4, 5, -5, 6, -6, 7, -7, 8)
GROUPS = 4
PER_GROUP = NZ // GROUPS
GROUP_ROWS = PER_GROUP * ROWS
XY = NX * NY
NT = (((1,), (1,)), ((), ()))


def slot_of(offset):
    return Z_SLOTS.index(offset if offset != -8 else 8)


def device_at(dx, dy, dz, dc):
    wide = lax.axis_index("wide")
    grp = lax.axis_index("grp")
    x = (wide // 16 + dx) % NX
    y = ((wide // 4) % 4 + dy) % NY
    z = ((wide % 4) * 4 + grp // 2 + dz) % NZ
    core = (grp % 2 + dc) % NC
    return (x * 16 + y * 4 + z // 4, (z % 4) * 2 + core)


def remote(src, dst, send_sem, recv_sem, where):
    return pltpu.make_async_remote_copy(
        src_ref=src,
        dst_ref=dst,
        send_sem=send_sem,
        recv_sem=recv_sem,
        device_id=device_at(*where),
        device_id_type=MESH,
    )


def kernel(
    samples_hbm,
    archive_hbm,
    inv_hbm,
    mean_hbm,
    var_hbm,
    out_ref,
    own_raw,
    arch_raw,
    inv,
    coef,
    arch,
    arch_half,
    z_in,
    z_wide,
    main,
    part,
    part_own,
    xy_in,
    z_out,
    z_back,
    load_sem,
    swap_send,
    swap_recv,
    z_send,
    z_recv,
    one_send,
    one_recv,
    two_send,
    two_recv,
    xy_send,
    xy_recv,
    back_send,
    back_recv,
):
    z_partners = [(0, 0, d, 0) for d in Z_SLOTS[1:]]
    xy_partners = [(a, b, 0, 0) for a in range(NX) for b in range(NY) if a or b]
    partners = z_partners + xy_partners + [(0, 0, 0, 1)]
    barrier = pltpu.get_barrier_semaphore()
    for where in partners:
        pl.semaphore_signal(barrier, inc=1, device_id=device_at(*where), device_id_type=MESH)

    loads = [
        pltpu.make_async_copy(samples_hbm, own_raw, load_sem.at[0]),
        pltpu.make_async_copy(inv_hbm, inv, load_sem.at[1]),
        pltpu.make_async_copy(archive_hbm, arch_raw, load_sem.at[2]),
        pltpu.make_async_copy(mean_hbm, coef.at[0, pl.ds(0, OUT), pl.ds(0, RUNS)], load_sem.at[3]),
        pltpu.make_async_copy(var_hbm, coef.at[1, pl.ds(OUT, OUT), pl.ds(0, RUNS)], load_sem.at[4]),
    ]
    for load in loads:
        load.start()
    coef[0, OUT : 2 * OUT, :] = jnp.zeros((OUT, 2 * RUNS), BF16)
    coef[1, 0:OUT, :] = jnp.zeros((OUT, 2 * RUNS), BF16)
    loads[0].wait()
    loads[1].wait()
    factor = inv[...] * DIN ** (-0.5)
    z_in[0] = (own_raw[...].astype(F32) * factor).astype(BF16)
    loads[2].wait()
    scaled = (arch_raw[...].astype(F32) * factor).astype(BF16)
    arch[0:RUNS, :] = scaled
    wide_copy = scaled.astype(F32)
    half_norm = 0.5 * jnp.sum(wide_copy * wide_copy, axis=-1, keepdims=True)
    arch_half[:, 0:RUNS] = jnp.transpose(jnp.broadcast_to(half_norm, (RUNS, 128)))[0:8, :]
    loads[3].wait()
    loads[4].wait()

    pl.semaphore_wait(barrier, len(partners))

    for slot in range(NZ - 1, 0, -1):
        there = slot_of(-Z_SLOTS[slot])
        remote(
            z_in.at[0], z_in.at[there], z_send.at[0], z_recv.at[there // PER_GROUP], (0, 0, Z_SLOTS[slot], 0)
        ).start()
    here, other = pl.ds(0, RUNS), pl.ds(RUNS, RUNS)
    low, high = pl.ds(0, OUT), pl.ds(OUT, OUT)
    swap = [
        remote(arch.at[here], arch.at[other], swap_send.at[0], swap_recv.at[0], (0, 0, 0, 1)),
        remote(arch_half.at[:, here], arch_half.at[:, other], swap_send.at[1], swap_recv.at[1], (0, 0, 0, 1)),
        remote(coef.at[0, low, here], coef.at[0, low, other], swap_send.at[2], swap_recv.at[2], (0, 0, 0, 1)),
        remote(coef.at[1, high, here], coef.at[1, high, other], swap_send.at[3], swap_recv.at[3], (0, 0, 0, 1)),
    ]
    for copy in swap:
        copy.start()

    rest = pl.ds(1, 3)

    def y_first(group):
        return group % 2 == 0

    def from_z(group):
        first = max(1, group * PER_GROUP)
        landed = z_in.at[pl.ds(first, (group + 1) * PER_GROUP - first)]
        remote(landed, landed, z_send.at[0], z_recv.at[group], (0, 0, 1, 0)).wait_recv()
        for place in range(PER_GROUP):
            z_wide[place * ROWS : (place + 1) * ROWS, :] = z_in[group * PER_GROUP + place].astype(F32)
        main[group, 0, 0] = z_wide[...].astype(BF16)
        for step in (1, 2, 3):
            back = 4 - step
            target = main.at[group, 0, back] if y_first(group) else main.at[group, back, 0]
            where = (0, step, 0, 0) if y_first(group) else (step, 0, 0, 0)
            remote(main.at[group, 0, 0], target, one_send.at[group], one_recv.at[group], where).start()

    def landed_one(group):
        return main.at[group, 0, rest] if y_first(group) else main.at[group, rest, 0]

    def landed_two(group):
        return main.at[group, rest] if y_first(group) else main.at[group, :, rest]

    def second(group):
        landed = landed_one(group)
        remote(landed, landed, one_send.at[group], one_recv.at[group], (1, 0, 0, 0)).wait_recv()
        for step in (1, 2, 3):
            back = 4 - step
            source = main.at[group, 0] if y_first(group) else main.at[group, :, 0]
            target = main.at[group, back] if y_first(group) else main.at[group, :, back]
            where = (step, 0, 0, 0) if y_first(group) else (0, step, 0, 0)
            remote(source, target, two_send.at[group], two_recv.at[group], where).start()

    def compute(group):
        landed = landed_two(group)
        remote(landed, landed, two_send.at[group], two_recv.at[group], (1, 0, 0, 0)).wait_recv()
        block = main[group].reshape(XY * GROUP_ROWS, DIN)
        wide_block = block.astype(F32)
        samp_half = 0.5 * jnp.sum(wide_block * wide_block, axis=-1, keepdims=True)
        inner = lax.dot_general(block, arch[...], NT, preferred_element_type=F32)
        value = jnp.exp(inner - samp_half - arch_half[0:1, :])
        total = lax.dot_general(value.astype(BF16), coef[0], NT, preferred_element_type=F32)
        total = total + lax.dot_general((value * value).astype(BF16), coef[1], NT, preferred_element_type=F32)
        part_own[group] = total[0:GROUP_ROWS, :]
        part[group] = total.astype(BF16).reshape(XY, GROUP_ROWS, 2 * OUT)
        for spot in range(1, XY):
            a, b = spot // NY, spot % NY
            there = ((NX - a) % NX) * NY + (NY - b) % NY
            remote(
                part.at[group, spot], xy_in.at[group, there], xy_send.at[group], xy_recv.at[group], (a, b, 0, 0)
            ).start()

    def reduce_xy(group):
        landed = xy_in.at[group, pl.ds(1, XY - 1)]
        remote(landed, landed, xy_send.at[group], xy_recv.at[group], (1, 0, 0, 0)).wait_recv()
        total = part_own[group] + jnp.sum(xy_in[group, 1:XY].astype(F32), axis=0)
        for place in range(PER_GROUP):
            slot = group * PER_GROUP + place
            z_out[slot] = total[place * ROWS : (place + 1) * ROWS, :]
            if slot:
                there = slot_of(-Z_SLOTS[slot])
                remote(
                    z_out.at[slot], z_back.at[there], back_send.at[0], back_recv.at[0], (0, 0, Z_SLOTS[slot], 0)
                ).start()

    from_z(0)
    from_z(1)
    from_z(2)
    second(0)
    from_z(3)
    second(1)
    second(2)
    for copy in swap:
        copy.wait_recv()
    compute(0)
    second(3)
    compute(1)
    compute(2)
    compute(3)
    for group in range(GROUPS):
        reduce_xy(group)

    landed = z_back.at[pl.ds(1, NZ - 1)]
    remote(landed, landed, back_send.at[0], back_recv.at[0], (0, 0, 1, 0)).wait_recv()
    out_ref[...] = z_out[0] + jnp.sum(z_back[1:NZ], axis=0)

    sent = z_in.at[pl.ds(1, NZ - 1)]
    remote(sent, sent, z_send.at[0], z_recv.at[0], (0, 0, 1, 0)).wait_send()
    for copy in swap:
        copy.wait_send()
    for group in range(GROUPS):
        one, two, three = landed_one(group), landed_two(group), xy_in.at[group, pl.ds(1, XY - 1)]
        remote(one, one, one_send.at[group], one_recv.at[group], (1, 0, 0, 0)).wait_send()
        remote(two, two, two_send.at[group], two_recv.at[group], (1, 0, 0, 0)).wait_send()
        remote(three, three, xy_send.at[group], xy_recv.at[group], (1, 0, 0, 0)).wait_send()
    remote(landed, landed, back_send.at[0], back_recv.at[0], (0, 0, 1, 0)).wait_send()


def on_device(samples, archive, inv_len, mean_coef, var_coef):
    dma = pltpu.SemaphoreType.DMA
    sums = pl.pallas_call(
        kernel,
        out_shape=jax.ShapeDtypeStruct((ROWS, 2 * OUT), F32),
        in_specs=[pl.BlockSpec(memory_space=pl.ANY)] * 5,
        out_specs=pl.BlockSpec(memory_space=pltpu.VMEM),
        scratch_shapes=[
            pltpu.VMEM((ROWS, DIN), BF16),
            pltpu.VMEM((RUNS, DIN), BF16),
            pltpu.VMEM((1, DIN), F32),
            pltpu.VMEM((2, 2 * OUT, 2 * RUNS), BF16),
            pltpu.VMEM((2 * RUNS, DIN), BF16),
            pltpu.VMEM((8, 2 * RUNS), F32),
            pltpu.VMEM((NZ, ROWS, DIN), BF16),
            pltpu.VMEM((GROUP_ROWS, DIN), F32),
            pltpu.VMEM((GROUPS, NX, NY, GROUP_ROWS, DIN), BF16),
            pltpu.VMEM((GROUPS, XY, GROUP_ROWS, 2 * OUT), BF16),
            pltpu.VMEM((GROUPS, GROUP_ROWS, 2 * OUT), F32),
            pltpu.VMEM((GROUPS, XY, GROUP_ROWS, 2 * OUT), BF16),
            pltpu.VMEM((NZ, ROWS, 2 * OUT), F32),
            pltpu.VMEM((NZ, ROWS, 2 * OUT), F32),
            dma((5,)),
            dma((4,)),
            dma((4,)),
            dma((1,)),
            dma((GROUPS,)),
            dma((GROUPS,)),
            dma((GROUPS,)),
            dma((GROUPS,)),
            dma((GROUPS,)),
            dma((GROUPS,)),
            dma((GROUPS,)),
            dma((1,)),
            dma((1,)),
        ],
        name="surrogate",
        compiler_params=pltpu.CompilerParams(
            collective_id=0, has_side_effects=True, vmem_limit_bytes=60 << 20
        ),
    )(samples, archive, inv_len.reshape(1, DIN), mean_coef.T, var_coef.T)
    return (sums[:, :OUT], 1.0 - sums[:, OUT:])


def solution(mesh):
    rows = P(("wide", "grp"), None)
    return jax.shard_map(
        on_device,
        mesh=mesh,
        in_specs=(rows, rows, P(), rows, rows),
        out_specs=(rows, rows),
        check_vma=False,
    )
```

time: 717 us -> 52.2 us (0.07)
  the two profiles are of different devices: /device:TPU:1 before, /device:TPU:4 now
where the time goes in v1:
time: 52.2 us; the launch traced here: 52.1 us
  Pallas kernels  50 us (96%)
  other arithmetic  1.4 us (3%)
  between operations  0.64 us (1%)
    pallas_call x1, Pallas kernels, on_device(): pl.pallas_call(kernel, out_shape=jax.ShapeDtypeStruct((ROWS, 2 * OUT), F3...  50 us
    sub x1, other arithmetic, on_device(): return (sums[:, :OUT], 1.0 - sums[:, OUT:])  1.4 us

profile of v1, /device:TPU:4, one launch (start us, length us, event | category | flops | bytes accessed | tf_op | source)
XLA Modules:
  0.0 52.1 jit_solution(3612667779671651552)
XLA Ops:
  0.6 50.0 %surrogate.1 = f32[4,128]{1,0:T(4,128)} custom-call(bf16[4,512]{1,0:T(4,128)(2,1)} %samples_hbm.1, bf16[512,512]{1,0:T(8,128)(2,1)} %archive_hbm.1, f32[1,512]{1,0:T(1,128)} %bitcast.5, bf16[64,512]{1,0:T(8,128)(2,1)} %bitcast.3, bf16[64,512]{1,0:T(8,128)(2,1)} %bitcast.4), custom_call_target="tpu_custom_call" | custom-call | tf_op jit(solution)/shard_map/surrogate/pallas_call | solution.py:236
  50.7 1.4 %slice_subtract_fusion = (f32[4,64]{1,0:T(4,128)}, f32[4,64]{1,0:T(4,128)}) fusion(f32[4,128]{1,0:T(4,128)} %surrogate.1), kind=kLoop, calls=%fused_computation | loop fusion | flops 256 | bytes 4096 | tf_op jit(solution)/shard_map/sub | solution.py:275

commit v2 on v1

--- a/solution.py
+++ b/solution.py
@@ -15,8 +15,14 @@
 ROWS = 4
 RUNS = 512
 NX, NY, NZ, NC = 4, 4, 16, 2
-Z_SLOTS = (0, 1, -1, 2, -2, 3, -3, 4, -4, 5, -5, 6, -6, 7, -7, 8)
+Z_SLOTS = (0, 1, 2, 3, 4, -1, -2, -3, -4, 5, 6, 7, 8, -5, -6, -7)
+NEAR = (4, -4, 3, -3, 2, -2, 1, -1)
 GROUPS = 4
+DIRECT = (2, 3)
+FAR_STEPS = (
+    (2, 2), (2, 1), (2, 3), (1, 2), (3, 2), (2, 0), (0, 2), (1, 1),
+    (1, 3), (3, 1), (3, 3), (1, 0), (3, 0), (0, 1), (0, 3),
+)
 PER_GROUP = NZ // GROUPS
 GROUP_ROWS = PER_GROUP * ROWS
 XY = NX * NY
@@ -83,7 +89,7 @@
     back_send,
     back_recv,
 ):
-    z_partners = [(0, 0, d, 0) for d in Z_SLOTS[1:]]
+    z_partners = [(0, 0, d, 0) for d in NEAR]
     xy_partners = [(a, b, 0, 0) for a in range(NX) for b in range(NY) if a or b]
     partners = z_partners + xy_partners + [(0, 0, 0, 1)]
     barrier = pltpu.get_barrier_semaphore()
@@ -99,12 +105,17 @@
     ]
     for load in loads:
         load.start()
-    coef[0, OUT : 2 * OUT, :] = jnp.zeros((OUT, 2 * RUNS), BF16)
-    coef[1, 0:OUT, :] = jnp.zeros((OUT, 2 * RUNS), BF16)
     loads[0].wait()
     loads[1].wait()
     factor = inv[...] * DIN ** (-0.5)
     z_in[0] = (own_raw[...].astype(F32) * factor).astype(BF16)
+    pl.semaphore_wait(barrier, len(partners))
+
+    up, down, edge, far_up, far_down = [pl.ds(*span) for span in ((1, 4), (5, 3), (8, 1), (9, 4), (13, 3))]
+    for offset in NEAR:
+        there = slot_of(-offset)
+        kind = 2 if there == 8 else 0 if there < 5 else 1
+        remote(z_in.at[0], z_in.at[there], z_send.at[0], z_recv.at[kind], (0, 0, offset, 0)).start()
     loads[2].wait()
     scaled = (arch_raw[...].astype(F32) * factor).astype(BF16)
     arch[0:RUNS, :] = scaled
@@ -113,14 +124,8 @@
     arch_half[:, 0:RUNS] = jnp.transpose(jnp.broadcast_to(half_norm, (RUNS, 128)))[0:8, :]
     loads[3].wait()
     loads[4].wait()
-
-    pl.semaphore_wait(barrier, len(partners))
-
-    for slot in range(NZ - 1, 0, -1):
-        there = slot_of(-Z_SLOTS[slot])
-        remote(
-            z_in.at[0], z_in.at[there], z_send.at[0], z_recv.at[there // PER_GROUP], (0, 0, Z_SLOTS[slot], 0)
-        ).start()
+    coef[0, OUT : 2 * OUT, :] = jnp.zeros((OUT, 2 * RUNS), BF16)
+    coef[1, 0:OUT, :] = jnp.zeros((OUT, 2 * RUNS), BF16)
     here, other = pl.ds(0, RUNS), pl.ds(RUNS, RUNS)
     low, high = pl.ds(0, OUT), pl.ds(OUT, OUT)
     swap = [
@@ -137,13 +142,24 @@
     def y_first(group):
         return group % 2 == 0
 
+    def z_landed(span, kind):
+        landed = z_in.at[span]
+        remote(landed, landed, z_send.at[0], z_recv.at[kind], (0, 0, 1, 0)).wait_recv()
+
+    def z_relay(span, target, kind, offset):
+        remote(z_in.at[span], z_in.at[target], z_send.at[0], z_recv.at[kind], (0, 0, offset, 0)).start()
+
     def from_z(group):
-        first = max(1, group * PER_GROUP)
-        landed = z_in.at[pl.ds(first, (group + 1) * PER_GROUP - first)]
-        remote(landed, landed, z_send.at[0], z_recv.at[group], (0, 0, 1, 0)).wait_recv()
         for place in range(PER_GROUP):
             z_wide[place * ROWS : (place + 1) * ROWS, :] = z_in[group * PER_GROUP + place].astype(F32)
         main[group, 0, 0] = z_wide[...].astype(BF16)
+        if group in DIRECT:
+            for a, b in FAR_STEPS:
+                target = main.at[group, (4 - a) % 4, (4 - b) % 4]
+                later = a if y_first(group) else b
+                sends, receives = (two_send, two_recv) if later else (one_send, one_recv)
+                remote(main.at[group, 0, 0], target, sends.at[group], receives.at[group], (a, b, 0, 0)).start()
+            return
         for step in (1, 2, 3):
             back = 4 - step
             target = main.at[group, 0, back] if y_first(group) else main.at[group, back, 0]
@@ -157,6 +173,8 @@
         return main.at[group, rest] if y_first(group) else main.at[group, :, rest]
 
     def second(group):
+        if group in DIRECT:
+            return
         landed = landed_one(group)
         remote(landed, landed, one_send.at[group], one_recv.at[group], (1, 0, 0, 0)).wait_recv()
         for step in (1, 2, 3):
@@ -168,6 +186,9 @@
 
     def compute(group):
         landed = landed_two(group)
+        if group in DIRECT:
+            one = landed_one(group)
+            remote(one, one, one_send.at[group], one_recv.at[group], (1, 0, 0, 0)).wait_recv()
         remote(landed, landed, two_send.at[group], two_recv.at[group], (1, 0, 0, 0)).wait_recv()
         block = main[group].reshape(XY * GROUP_ROWS, DIN)
         wide_block = block.astype(F32)
@@ -178,8 +199,8 @@
         total = total + lax.dot_general((value * value).astype(BF16), coef[1], NT, preferred_element_type=F32)
         part_own[group] = total[0:GROUP_ROWS, :]
         part[group] = total.astype(BF16).reshape(XY, GROUP_ROWS, 2 * OUT)
-        for spot in range(1, XY):
-            a, b = spot // NY, spot % NY
+        for a, b in FAR_STEPS:
+            spot = a * NY + b
             there = ((NX - a) % NX) * NY + (NY - b) % NY
             remote(
                 part.at[group, spot], xy_in.at[group, there], xy_send.at[group], xy_recv.at[group], (a, b, 0, 0)
@@ -198,17 +219,23 @@
                     z_out.at[slot], z_back.at[there], back_send.at[0], back_recv.at[0], (0, 0, Z_SLOTS[slot], 0)
                 ).start()
 
+    z_landed(up, 0)
+    z_relay(up, far_up, 3, -4)
+    z_landed(down, 1)
+    z_relay(down, far_down, 4, 4)
     from_z(0)
     from_z(1)
+    second(0)
+    second(1)
+    z_landed(edge, 2)
+    z_landed(far_up, 3)
     from_z(2)
-    second(0)
+    z_landed(far_down, 4)
     from_z(3)
-    second(1)
     second(2)
     for copy in swap:
         copy.wait_recv()
     compute(0)
-    second(3)
     compute(1)
     compute(2)
     compute(3)
@@ -257,7 +284,7 @@
             dma((4,)),
             dma((4,)),
             dma((1,)),
-            dma((GROUPS,)),
+            dma((5,)),
             dma((GROUPS,)),
             dma((GROUPS,)),
             dma((GROUPS,)),
@@ -269,9 +296,9 @@
         ],
         name="surrogate",
         compiler_params=pltpu.CompilerParams(
-            collective_id=0, has_side_effects=True, vmem_limit_bytes=60 << 20
+            collective_id=0, has_side_effects=True, vmem_limit_bytes=32 << 20
         ),
-    )(samples, archive, inv_len.reshape(1, DIN), mean_coef.T, var_coef.T)
+    )(*[pltpu.with_memory_space_constraint(a, pltpu.HBM) for a in (samples, archive, inv_len.reshape(1, DIN), mean_coef.T, var_coef.T)])
     return (sums[:, :OUT], 1.0 - sums[:, OUT:])
 
 

time: 52.2 us -> 47 us (0.900)
  the two profiles are of different devices: /device:TPU:4 before, /device:TPU:8 now
where the time goes in v2:
time: 47 us; the launch traced here: 46.9 us
  Pallas kernels  45.6 us (97%)
  other arithmetic  0.65 us (1%)
  between operations  0.64 us (1%)
    pallas_call x1, Pallas kernels, on_device(): pl.pallas_call(kernel, out_shape=jax.ShapeDtypeStruct((ROWS, 2 * OUT), F3...  45.6 us

profile of v2, /device:TPU:8, one launch (start us, length us, event | category | flops | bytes accessed | tf_op | source)
XLA Modules:
  0.0 46.9 jit_solution(6020539753177830242)
XLA Ops:
  0.6 45.6 %surrogate.1 = f32[4,128]{1,0:T(4,128)S(1)} custom-call(bf16[4,512]{1,0:T(4,128)(2,1)} %samples_hbm.1, bf16[512,512]{1,0:T(8,128)(2,1)} %archive_hbm.1, f32[1,512]{1,0:T(1,128)} %bitcast.5, bf16[64,512]{1,0:T(8,128)(2,1)} %bitcast.3, bf16[64,512]{1,0:T(8,128)(2,1)} %bitcast.4), custom_call_target="tpu_custom_call" | custom-call | tf_op jit(solution)/shard_map/surrogate/pallas_call | solution.py:263
  46.2 0.7 %slice_subtract_fusion = (f32[4,64]{1,0:T(4,128)}, f32[4,64]{1,0:T(4,128)}) fusion(f32[4,128]{1,0:T(4,128)S(1)} %surrogate.1), kind=kLoop, calls=%fused_computation | loop fusion | flops 256 | bytes 4096 | tf_op jit(solution)/shard_map/sub | solution.py:302

commit v3 on v2

v3 whole, which is shorter than its diff:
```python
import functools

import jax
import jax.numpy as jnp
from jax import lax
from jax.experimental import pallas as pl
from jax.experimental.pallas import tpu as pltpu
from jax.sharding import PartitionSpec as P

MESH = pl.DeviceIdType.MESH
F32 = jnp.float32
BF16 = jnp.bfloat16
DIN = 512
OUT = 64
ROWS = 4
RUNS = 512
NX, NY, NZ, NC = 4, 4, 16, 2
Z_SLOTS = (0, 1, 2, 3, 4, -1, -2, -3, -4, 5, 6, 7, 8, -5, -6, -7)
NEAR = (4, -4, 3, -3, 2, -2, 1, -1)
GROUPS = 4
LEAF, HUB = 0, 1
EXTRA = GROUPS
JOBS = GROUPS + 1
WORK = ((2, 0, 1), (2, 3, EXTRA, 0, 1))
DIRECT = (2, 3, EXTRA)
FAR_STEPS = (
    (2, 2), (2, 1), (2, 3), (1, 2), (3, 2), (2, 0), (0, 2), (1, 1),
    (1, 3), (3, 1), (3, 3), (1, 0), (3, 0), (0, 1), (0, 3),
)
PER_GROUP = NZ // GROUPS
GROUP_ROWS = PER_GROUP * ROWS
XY = NX * NY
NT = (((1,), (1,)), ((), ()))


def slot_of(offset):
    return Z_SLOTS.index(offset if offset != -8 else 8)


def device_at(dx, dy, dz, core):
    wide = lax.axis_index("wide")
    grp = lax.axis_index("grp")
    x = (wide // 16 + dx) % NX
    y = ((wide // 4) % 4 + dy) % NY
    z = ((wide % 4) * 4 + grp // 2 + dz) % NZ
    return (x * 16 + y * 4 + z // 4, (z % 4) * 2 + core)


def remote(src, dst, send_sem, recv_sem, where):
    return pltpu.make_async_remote_copy(
        src_ref=src,
        dst_ref=dst,
        send_sem=send_sem,
        recv_sem=recv_sem,
        device_id=device_at(*where),
        device_id_type=MESH,
    )


def kernel(
    samples_hbm,
    archive_hbm,
    inv_hbm,
    mean_hbm,
    var_hbm,
    out_ref,
    own_raw,
    own_z,
    arch_raw,
    inv,
    coef,
    arch,
    arch_half,
    z_in,
    z_wide,
    main,
    part,
    part_own,
    xy_in,
    z_out,
    z_back,
    load_sem,
    swap_send,
    swap_recv,
    z_send,
    z_recv,
    one_send,
    one_recv,
    two_send,
    two_recv,
    xy_send,
    xy_recv,
    back_send,
    back_recv,
):
    core = lax.axis_index("grp") % NC
    barrier = pltpu.get_barrier_semaphore()

    def partners_of(me):
        return [(0, 0, d, me) for d in NEAR] + [(a, b, 0, me) for a, b in FAR_STEPS] + [(0, 0, 0, 1 - me)]

    for me in (LEAF, HUB):

        @pl.when(core == me)
        def _():
            for where in partners_of(me):
                pl.semaphore_signal(barrier, inc=1, device_id=device_at(*where), device_id_type=MESH)

    loads = [
        pltpu.make_async_copy(samples_hbm, own_raw, load_sem.at[0]),
        pltpu.make_async_copy(inv_hbm, inv, load_sem.at[1]),
        pltpu.make_async_copy(archive_hbm, arch_raw, load_sem.at[2]),
        pltpu.make_async_copy(mean_hbm, coef.at[0, pl.ds(0, OUT), pl.ds(0, RUNS)], load_sem.at[3]),
        pltpu.make_async_copy(var_hbm, coef.at[1, pl.ds(OUT, OUT), pl.ds(0, RUNS)], load_sem.at[4]),
    ]
    for load in loads:
        load.start()
    loads[0].wait()
    loads[1].wait()
    factor = inv[...] * DIN ** (-0.5)
    own_z[...] = (own_raw[...].astype(F32) * factor).astype(BF16)
    up, down, edge, far_up, far_down = [pl.ds(*span) for span in ((1, 4), (5, 3), (8, 1), (9, 4), (13, 3))]
    up_most, last_up, far_most, last_far = pl.ds(1, 3), pl.ds(4, 1), pl.ds(9, 3), pl.ds(12, 1)

    def send_own(me):
        pl.semaphore_wait(barrier, len(partners_of(me)))
        for offset in NEAR:
            there = slot_of(-offset)
            kind = 2 if there == 8 else 0 if there < 5 else 1
            remote(own_z, z_in.at[there, me], z_send.at[0], z_recv.at[kind], (0, 0, offset, me)).start()
        z_in[0, me] = own_z[...]

    def prepare():
        loads[2].wait()
        scaled = (arch_raw[...].astype(F32) * factor).astype(BF16)
        arch[0:RUNS, :] = scaled
        wide_copy = scaled.astype(F32)
        half_norm = 0.5 * jnp.sum(wide_copy * wide_copy, axis=-1, keepdims=True)
        arch_half[:, 0:RUNS] = jnp.transpose(jnp.broadcast_to(half_norm, (RUNS, 128)))[0:8, :]
        loads[3].wait()
        loads[4].wait()
        coef[0, OUT : 2 * OUT, :] = jnp.zeros((OUT, 2 * RUNS), BF16)
        coef[1, 0:OUT, :] = jnp.zeros((OUT, 2 * RUNS), BF16)

    here, other = pl.ds(0, RUNS), pl.ds(RUNS, RUNS)
    low, high = pl.ds(0, OUT), pl.ds(OUT, OUT)

    def swap_of(me):
        where = (0, 0, 0, 1 - me)
        return [
            remote(arch.at[here], arch.at[other], swap_send.at[0], swap_recv.at[0], where),
            remote(arch_half.at[:, here], arch_half.at[:, other], swap_send.at[1], swap_recv.at[1], where),
            remote(coef.at[0, low, here], coef.at[0, low, other], swap_send.at[2], swap_recv.at[2], where),
            remote(coef.at[1, high, here], coef.at[1, high, other], swap_send.at[3], swap_recv.at[3], where),
        ]

    rest = pl.ds(1, 3)

    def y_first(group):
        return group % 2 == 0

    def z_landed(span, half, kind):
        landed = z_in.at[span, half]
        remote(landed, landed, z_send.at[0], z_recv.at[kind], (0, 0, 1, HUB)).wait_recv()

    def z_relay(span, target, half, kind, offset, core_there):
        remote(
            z_in.at[span, half], z_in.at[target, half], z_send.at[0], z_recv.at[kind], (0, 0, offset, core_there)
        ).start()

    def from_z(group, me):
        half, first = (LEAF, NZ - PER_GROUP) if group == EXTRA else (me, group * PER_GROUP)
        for place in range(PER_GROUP):
            z_wide[place * ROWS : (place + 1) * ROWS, :] = z_in[first + place, half].astype(F32)
        main[group, 0, 0] = z_wide[...].astype(BF16)
        for a, b in FAR_STEPS:
            later = a if y_first(group) else b
            if later and group not in DIRECT:
                continue
            target = main.at[group, (4 - a) % 4, (4 - b) % 4]
            sends, receives = (two_send, two_recv) if later else (one_send, one_recv)
            remote(main.at[group, 0, 0], target, sends.at[group], receives.at[group], (a, b, 0, me)).start()

    def landed_one(group):
        return main.at[group, 0, rest] if y_first(group) else main.at[group, rest, 0]

    def landed_two(group):
        return main.at[group, rest] if y_first(group) else main.at[group, :, rest]

    def second(group, me):
        landed = landed_one(group)
        remote(landed, landed, one_send.at[group], one_recv.at[group], (1, 0, 0, 0)).wait_recv()
        for step in (1, 2, 3):
            back = 4 - step
            source = main.at[group, 0] if y_first(group) else main.at[group, :, 0]
            target = main.at[group, back] if y_first(group) else main.at[group, :, back]
            where = (step, 0, 0, me) if y_first(group) else (0, step, 0, me)
            remote(source, target, two_send.at[group], two_recv.at[group], where).start()

    def compute(group, me):
        landed = landed_two(group)
        if group in DIRECT:
            one = landed_one(group)
            remote(one, one, one_send.at[group], one_recv.at[group], (1, 0, 0, 0)).wait_recv()
        remote(landed, landed, two_send.at[group], two_recv.at[group], (1, 0, 0, 0)).wait_recv()
        block = main[group].reshape(XY * GROUP_ROWS, DIN)
        wide_block = block.astype(F32)
        samp_half = 0.5 * jnp.sum(wide_block * wide_block, axis=-1, keepdims=True)
        inner = lax.dot_general(block, arch[...], NT, preferred_element_type=F32)
        value = jnp.exp(inner - samp_half - arch_half[0:1, :])
        total = lax.dot_general(value.astype(BF16), coef[0], NT, preferred_element_type=F32)
        total = total + lax.dot_general((value * value).astype(BF16), coef[1], NT, preferred_element_type=F32)
        part_own[group] = total[0:GROUP_ROWS, :]
        part[group] = total.astype(BF16).reshape(XY, GROUP_ROWS, 2 * OUT)
        for a, b in FAR_STEPS:
            spot = a * NY + b
            there = ((NX - a) % NX) * NY + (NY - b) % NY
            remote(
                part.at[group, spot], xy_in.at[group, there], xy_send.at[group], xy_recv.at[group], (a, b, 0, me)
            ).start()

    def reduce_xy(group, me):
        landed = xy_in.at[group, pl.ds(1, XY - 1)]
        remote(landed, landed, xy_send.at[group], xy_recv.at[group], (1, 0, 0, 0)).wait_recv()
        total = part_own[group] + jnp.sum(xy_in[group, 1:XY].astype(F32), axis=0)
        half, first = (LEAF, NZ - PER_GROUP) if group == EXTRA else (me, group * PER_GROUP)
        for place in range(PER_GROUP):
            slot = first + place
            piece = total[place * ROWS : (place + 1) * ROWS, :]
            if slot == 0:
                z_back[0] = piece
                continue
            leaving = group * PER_GROUP + place
            z_out[leaving] = piece
            remote(
                z_out.at[leaving],
                z_back.at[slot_of(-Z_SLOTS[slot])],
                back_send.at[0],
                back_recv.at[0],
                (0, 0, Z_SLOTS[slot], half),
            ).start()

    def run(me):
        jobs = WORK[me]
        send_own(me)
        prepare()
        swap = swap_of(me)
        for copy in swap:
            copy.start()
        z_landed(up, me, 0)
        if me == HUB:
            z_relay(up, far_up, me, 3, -4, HUB)
            z_landed(down, me, 1)
            z_relay(down, far_down, me, 4, 4, HUB)
            z_landed(edge, me, 2)
        else:
            z_relay(up_most, far_most, me, 3, -4, LEAF)
            z_landed(edge, me, 2)
            z_relay(last_up, last_far, me, 5, -4, HUB)
            z_landed(down, me, 1)
            z_relay(down, far_down, me, 6, 4, HUB)
        from_z(0, me)
        from_z(1, me)
        if me == HUB:
            z_landed(far_up, me, 3)
            from_z(2, me)
            z_landed(far_down, me, 4)
            from_z(3, me)
            z_landed(last_far, LEAF, 5)
            z_landed(far_down, LEAF, 6)
            from_z(EXTRA, me)
        else:
            z_landed(far_most, me, 3)
            from_z(2, me)
        second(0, me)
        second(1, me)
        for copy in swap:
            copy.wait_recv()
        for group in jobs:
            compute(group, me)
        for group in jobs:
            reduce_xy(group, me)
        landed = z_back.at[pl.ds(1, NZ - 1)]
        remote(landed, landed, back_send.at[0], back_recv.at[0], (0, 0, 1, me)).wait_recv()
        out_ref[...] = jnp.sum(z_back[...], axis=0)

        def drain(ref, sem):
            remote(ref, ref, sem, back_recv.at[0], (0, 0, 1, me)).wait_send()

        drain(z_in.at[pl.ds(1, NZ - 1), me], z_send.at[0])
        for copy in swap:
            copy.wait_send()
        for group in jobs:
            drain(landed_one(group), one_send.at[group])
            drain(landed_two(group), two_send.at[group])
            drain(xy_in.at[group, pl.ds(1, XY - 1)], xy_send.at[group])
        drain(z_out.at[pl.ds(1, len(jobs) * PER_GROUP - 1)], back_send.at[0])

    for me in (LEAF, HUB):

        @pl.when(core == me)
        def _():
            run(me)


def on_device(samples, archive, inv_len, mean_coef, var_coef):
    dma = pltpu.SemaphoreType.DMA
    sums = pl.pallas_call(
        kernel,
        out_shape=jax.ShapeDtypeStruct((ROWS, 2 * OUT), F32),
        in_specs=[pl.BlockSpec(memory_space=pl.ANY)] * 5,
        out_specs=pl.BlockSpec(memory_space=pltpu.VMEM),
        scratch_shapes=[
            pltpu.VMEM((ROWS, DIN), BF16),
            pltpu.VMEM((ROWS, DIN), BF16),
            pltpu.VMEM((RUNS, DIN), BF16),
            pltpu.VMEM((1, DIN), F32),
            pltpu.VMEM((2, 2 * OUT, 2 * RUNS), BF16),
            pltpu.VMEM((2 * RUNS, DIN), BF16),
            pltpu.VMEM((8, 2 * RUNS), F32),
            pltpu.VMEM((NZ, NC, ROWS, DIN), BF16),
            pltpu.VMEM((GROUP_ROWS, DIN), F32),
            pltpu.VMEM((JOBS, NX, NY, GROUP_ROWS, DIN), BF16),
            pltpu.VMEM((JOBS, XY, GROUP_ROWS, 2 * OUT), BF16),
            pltpu.VMEM((JOBS, GROUP_ROWS, 2 * OUT), F32),
            pltpu.VMEM((JOBS, XY, GROUP_ROWS, 2 * OUT), BF16),
            pltpu.VMEM((JOBS * PER_GROUP, ROWS, 2 * OUT), F32),
            pltpu.VMEM((NZ, ROWS, 2 * OUT), F32),
            dma((5,)),
            dma((4,)),
            dma((4,)),
            dma((1,)),
            dma((7,)),
            dma((JOBS,)),
            dma((JOBS,)),
            dma((JOBS,)),
            dma((JOBS,)),
            dma((JOBS,)),
            dma((JOBS,)),
            dma((1,)),
            dma((1,)),
        ],
        name="surrogate",
        compiler_params=pltpu.CompilerParams(
            collective_id=0, has_side_effects=True, vmem_limit_bytes=32 << 20
        ),
    )(*[pltpu.with_memory_space_constraint(a, pltpu.HBM) for a in (samples, archive, inv_len.reshape(1, DIN), mean_coef.T, var_coef.T)])
    return (sums[:, :OUT], 1.0 - sums[:, OUT:])


def solution(mesh):
    rows = P(("wide", "grp"), None)
    return jax.shard_map(
        on_device,
        mesh=mesh,
        in_specs=(rows, rows, P(), rows, rows),
        out_specs=(rows, rows),
        check_vma=False,
    )
```

time: 47 us -> 45.4 us (0.966)
  the two profiles are of different devices: /device:TPU:8 before, /device:TPU:1 now
where the time goes in v3:
time: 45.4 us; the launch traced here: 45.2 us
  Pallas kernels  43.9 us (97%)
  other arithmetic  0.65 us (1%)
  between operations  0.64 us (1%)
    pallas_call x1, Pallas kernels, on_device(): pl.pallas_call(kernel, out_shape=jax.ShapeDtypeStruct((ROWS, 2 * OUT), F3...  43.9 us

profile of v3, /device:TPU:1, one launch (start us, length us, event | category | flops | bytes accessed | tf_op | source)
XLA Modules:
  0.0 45.2 jit_solution(17332705952758416184)
XLA Ops:
  0.6 43.9 %surrogate.1 = f32[4,128]{1,0:T(4,128)S(1)} custom-call(bf16[4,512]{1,0:T(4,128)(2,1)} %samples_hbm.1, bf16[512,512]{1,0:T(8,128)(2,1)} %archive_hbm.1, f32[1,512]{1,0:T(1,128)} %bitcast.5, bf16[64,512]{1,0:T(8,128)(2,1)} %bitcast.3, bf16[64,512]{1,0:T(8,128)(2,1)} %bitcast.4), custom_call_target="tpu_custom_call" | custom-call | tf_op jit(solution)/shard_map/surrogate/pallas_call | solution.py:308
  44.5 0.7 %slice_subtract_fusion = (f32[4,64]{1,0:T(4,128)}, f32[4,64]{1,0:T(4,128)}) fusion(f32[4,128]{1,0:T(4,128)S(1)} %surrogate.1), kind=kLoop, calls=%fused_computation | loop fusion | flops 256 | bytes 4096 | tf_op jit(solution)/shard_map/sub | solution.py:348

commit v4 on v3

--- a/solution.py
+++ b/solution.py
@@ -97,7 +97,8 @@
     barrier = pltpu.get_barrier_semaphore()
 
     def partners_of(me):
-        return [(0, 0, d, me) for d in NEAR] + [(a, b, 0, me) for a, b in FAR_STEPS] + [(0, 0, 0, 1 - me)]
+        plane = [(a, b, 0, me) for a, b in FAR_STEPS if a == 0 or b == 0]
+        return [(0, 0, d, me) for d in NEAR] + plane + [(0, 0, 0, 1 - me)]
 
     for me in (LEAF, HUB):
 
@@ -187,9 +188,11 @@
     def landed_two(group):
         return main.at[group, rest] if y_first(group) else main.at[group, :, rest]
 
-    def second(group, me):
+    def first_landed(group):
         landed = landed_one(group)
         remote(landed, landed, one_send.at[group], one_recv.at[group], (1, 0, 0, 0)).wait_recv()
+
+    def second(group, me):
         for step in (1, 2, 3):
             back = 4 - step
             source = main.at[group, 0] if y_first(group) else main.at[group, :, 0]
@@ -261,6 +264,7 @@
             z_relay(down, far_down, me, 6, 4, HUB)
         from_z(0, me)
         from_z(1, me)
+        first_landed(0)
         if me == HUB:
             z_landed(far_up, me, 3)
             from_z(2, me)
@@ -273,6 +277,7 @@
             z_landed(far_most, me, 3)
             from_z(2, me)
         second(0, me)
+        first_landed(1)
         second(1, me)
         for copy in swap:
             copy.wait_recv()

time: 45.4 us -> 45.8 us (level)
  Pallas kernels: 43.9 us -> 44.4 us
where the time goes in v4:
time: 45.8 us; the launch traced here: 45.6 us
  Pallas kernels  44.4 us (97%)
  other arithmetic  0.65 us (1%)
  between operations  0.64 us (1%)
    pallas_call x1, Pallas kernels, on_device(): pl.pallas_call(kernel, out_shape=jax.ShapeDtypeStruct((ROWS, 2 * OUT), F3...  44.4 us

profile of v4, /device:TPU:1, one launch (start us, length us, event | category | flops | bytes accessed | tf_op | source)
XLA Modules:
  0.0 45.6 jit_solution(1278628654549597850)
XLA Ops:
  0.6 44.4 %surrogate.1 = f32[4,128]{1,0:T(4,128)S(1)} custom-call(bf16[4,512]{1,0:T(4,128)(2,1)} %samples_hbm.1, bf16[512,512]{1,0:T(8,128)(2,1)} %archive_hbm.1, f32[1,512]{1,0:T(1,128)} %bitcast.5, bf16[64,512]{1,0:T(8,128)(2,1)} %bitcast.3, bf16[64,512]{1,0:T(8,128)(2,1)} %bitcast.4), custom_call_target="tpu_custom_call" | custom-call | tf_op jit(solution)/shard_map/surrogate/pallas_call | solution.py:313
  45.0 0.7 %slice_subtract_fusion = (f32[4,64]{1,0:T(4,128)}, f32[4,64]{1,0:T(4,128)}) fusion(f32[4,128]{1,0:T(4,128)S(1)} %surrogate.1), kind=kLoop, calls=%fused_computation | loop fusion | flops 256 | bytes 4096 | tf_op jit(solution)/shard_map/sub | solution.py:353

commit v5 on v3

--- a/solution.py
+++ b/solution.py
@@ -272,12 +272,16 @@
         else:
             z_landed(far_most, me, 3)
             from_z(2, me)
-        second(0, me)
-        second(1, me)
+        if me == LEAF:
+            second(0, me)
+            second(1, me)
         for copy in swap:
             copy.wait_recv()
         for group in jobs:
             compute(group, me)
+            if group == 2 and me == HUB:
+                second(0, me)
+                second(1, me)
         for group in jobs:
             reduce_xy(group, me)
         landed = z_back.at[pl.ds(1, NZ - 1)]

time: 45.4 us -> 45.4 us (level)
  no operation moved by 1% of the time
where the time goes in v5:
time: 45.4 us; the launch traced here: 45.3 us
  Pallas kernels  44 us (97%)
  other arithmetic  0.65 us (1%)
  between operations  0.64 us (1%)
    pallas_call x1, Pallas kernels, on_device(): pl.pallas_call(kernel, out_shape=jax.ShapeDtypeStruct((ROWS, 2 * OUT), F3...  44 us

profile of v5, /device:TPU:1, one launch (start us, length us, event | category | flops | bytes accessed | tf_op | source)
XLA Modules:
  0.0 45.3 jit_solution(9847284111749870335)
XLA Ops:
  0.6 44.0 %surrogate.1 = f32[4,128]{1,0:T(4,128)S(1)} custom-call(bf16[4,512]{1,0:T(4,128)(2,1)} %samples_hbm.1, bf16[512,512]{1,0:T(8,128)(2,1)} %archive_hbm.1, f32[1,512]{1,0:T(1,128)} %bitcast.5, bf16[64,512]{1,0:T(8,128)(2,1)} %bitcast.3, bf16[64,512]{1,0:T(8,128)(2,1)} %bitcast.4), custom_call_target="tpu_custom_call" | custom-call | tf_op jit(solution)/shard_map/surrogate/pallas_call | solution.py:312
  44.7 0.7 %slice_subtract_fusion = (f32[4,64]{1,0:T(4,128)}, f32[4,64]{1,0:T(4,128)}) fusion(f32[4,128]{1,0:T(4,128)S(1)} %surrogate.1), kind=kLoop, calls=%fused_computation | loop fusion | flops 256 | bytes 4096 | tf_op jit(solution)/shard_map/sub | solution.py:352
